TPU v7x, 512 devices: a whole 4x8x8 slice. The times are simulated.
512 devices in a mesh: gx: 64 (over z, x, core), gy: 8 (over y).
Axes of the slice: x: 4, y: 8, z: 8, core: 2. Of those that a mesh axis runs over, the one named last changes fastest.
Arguments:
- velocity: float32 [3, 128, 1536, 128], P(None, 'gx', 'gy'), may hold values from -0.8 to 2.3
- stiffness: float32 [8], P('gy'), may hold values from 100 to 100000
- block_inverse: float32 [3, 1536, 192], P(None, 'gy'), as said below
Outputs:
- velocity_next: float32 [3, 128, 1536, 128], P(None, 'gx', 'gy')
Inputs may be any that keep to these rules, and one draw needn't show every extreme that they name: block_inverse[s] for block k is, to float32 rounding, the inverse of the 192-row matrix with 1 + 2 b on its diagonal and -b beside it, b = alpha_s stiffness[k].
All inputs are finite; a program needn't handle non-finite values.
Results may differ from a plain program's by a relative error of at most 0.0003.
Values sent between devices are 32-bit elements; how exact they have to be, the bound alone decides.
No kernel may reach another device: no remote copies, remote signals or barrier semaphores. Data moves between devices by JAX's collectives and lax.ppermute only.
A program may use at most 64 MiB of HBM per device.

v0:
```python
import jax
import jax.numpy as jnp
from jax import lax
from jax.sharding import PartitionSpec as P

SUBSTEPS = 3
implicit_share = (8.0 / 15.0, 2.0 / 15.0, 1.0 / 3.0)
new_weight = (8.0 / 15.0, 5.0 / 12.0, 3.0 / 4.0)
old_weight = (0.0, -17.0 / 60.0, -5.0 / 12.0)
courant = (0.3, 0.2, 0.3)


def with_halo(cells, sides, width, closed):
    for axis, dim in sides:
        count = lax.axis_size(axis)
        ends = count if closed else count - 1
        head = lax.slice_in_dim(cells, 0, width, axis=dim)
        tail = lax.slice_in_dim(cells, cells.shape[dim] - width, cells.shape[dim], axis=dim)
        cells = jnp.concatenate(
            [
                lax.ppermute(tail, axis, [(i, (i + 1) % count) for i in range(ends)]),
                cells,
                lax.ppermute(head, axis, [((i + 1) % count, i) for i in range(ends)]),
            ],
            axis=dim,
        )
    return cells


def upwind(field, back_two, back_one, ahead_one, ahead_two, speed):
    behind = 1.5 * field - 2.0 * back_one + 0.5 * back_two
    ahead = -1.5 * field + 2.0 * ahead_one - 0.5 * ahead_two
    return jnp.maximum(speed, 0.0) * behind + jnp.minimum(speed, 0.0) * ahead


def reduced(first_vals, last_vals, tips):
    count = first_vals.shape[0]
    prev_q = jnp.zeros((), jnp.float32)
    prev_last = jnp.zeros_like(first_vals[0])
    fronts, backs, front_qs, back_qs = ([], [], [], [])
    for block in range(count):
        head_v = tips[0][block]
        tail_v = tips[1][block]
        head_w = tips[2][block]
        tail_w = tips[3][block]
        pivot = 1.0 - head_v * prev_q
        front = (first_vals[block] - head_v * prev_last) / pivot
        back = last_vals[block] - tail_v * prev_last + tail_v * prev_q * front
        front_q = head_w / pivot
        back_q = tail_w + tail_v * prev_q * front_q
        fronts.append(front)
        backs.append(back)
        front_qs.append(front_q)
        back_qs.append(back_q)
        prev_q = back_q
        prev_last = back
    heads = [None] * count
    tails = [None] * count
    heads[count - 1] = fronts[count - 1]
    tails[count - 1] = backs[count - 1]
    for block in range(count - 2, -1, -1):
        after = heads[block + 1]
        heads[block] = fronts[block] - front_qs[block] * after
        tails[block] = backs[block] - back_qs[block] * after
    zero = jnp.zeros_like(first_vals[0])
    lower_prev = jnp.stack([zero] + tails[:-1])
    upper_next = jnp.stack(heads[1:] + [zero])
    return (lower_prev, upper_next)


def body(velocity, stiffness, block_inverse):
    blocks = lax.axis_size("gy")
    own_index = lax.axis_index("gy")
    spans = velocity.shape[3]
    stiff = stiffness[0]
    first_flag = (own_index > 0).astype(jnp.float32)
    last_flag = (own_index < blocks - 1).astype(jnp.float32)
    coupling = -jnp.array(implicit_share, jnp.float32) * stiff
    lower = coupling * first_flag
    upper = coupling * last_flag
    column_v = block_inverse[:, :, 0] * lower[:, None]
    column_w = block_inverse[:, :, -1] * upper[:, None]
    own_tips = jnp.stack(
        [column_v[:, 0], column_v[:, -1], column_w[:, 0], column_w[:, -1]], axis=1
    )[:, :, None]
    every_tip = lax.all_gather(own_tips, "gy", axis=2, tiled=True)
    current = velocity
    previous = velocity
    for step in range(SUBSTEPS):
        widened = with_halo(current, (("gx", 1),), 2, True)
        middle = widened[:, 2:-2]
        ypadded = with_halo(middle, (("gy", 2),), 2, False)
        along_x = upwind(
            middle,
            widened[:, 0:-4],
            widened[:, 1:-3],
            widened[:, 3:-1],
            widened[:, 4:],
            middle[0:1],
        )
        along_y = upwind(
            middle,
            ypadded[:, :, 0:-4],
            ypadded[:, :, 1:-3],
            ypadded[:, :, 3:-1],
            ypadded[:, :, 4:],
            middle[1:2],
        )
        along_z = upwind(
            middle,
            jnp.roll(middle, 2, 3),
            jnp.roll(middle, 1, 3),
            jnp.roll(middle, -1, 3),
            jnp.roll(middle, -2, 3),
            middle[2:3],
        )
        advect = courant[0] * along_x + courant[1] * along_y + courant[2] * along_z
        diffuse = stiff * (ypadded[:, :, 3:-1] - 2.0 * middle + ypadded[:, :, 1:-3])
        forcing = middle + implicit_share[step] * diffuse - new_weight[step] * advect
        if step > 0:
            forcing = forcing - old_weight[step] * previous
        previous = advect
        planes = middle.shape[1]
        solved = jnp.einsum(
            "ij,cxjz->cxiz", block_inverse[step], forcing, precision=lax.Precision.HIGHEST
        )
        edges = jnp.stack([solved[:, :, 0, :], solved[:, :, -1, :]]).reshape(2, -1)
        tips = every_tip[step]
        grouped = lax.all_to_all(
            edges.reshape(2, blocks, -1), "gy", split_axis=1, concat_axis=1, tiled=True
        )
        lower_prev, upper_next = reduced(grouped[0], grouped[1], tips)
        returned = lax.all_to_all(
            jnp.stack([lower_prev, upper_next]), "gy", split_axis=1, concat_axis=1, tiled=True
        ).reshape(2, -1)
        lower_own = returned[0]
        upper_own = returned[1]
        lower_own = lower_own.reshape(3, planes, spans)[:, :, None, :]
        upper_own = upper_own.reshape(3, planes, spans)[:, :, None, :]
        current = (
            solved
            - column_v[step][None, None, :, None] * lower_own
            - column_w[step][None, None, :, None] * upper_own
        )
    return current


def solution(mesh):
    return jax.shard_map(
        body,
        mesh=mesh,
        in_specs=(P(None, "gx", "gy", None), P("gy"), P(None, "gy", None)),
        out_specs=P(None, "gx", "gy", None),
        check_vma=False,
    )
```

profile of v0, /device:TPU:8, one launch (start us, length us, event | category | flops | bytes accessed | tf_op | source)
XLA Modules:
  0.0 241.1 jit_solution(6409454955614664541)
XLA Ops:
  0.0 12.6 %collective-permute-start.3 = (f32[3,2,192,128]{3,2,1,0:T(8,128)}, f32[3,2,192,128]{3,2,1,0:T(8,128)}, u32[]{:S(2)}, u32[]{:S(2)}) collective-permute-start(f32[3,2,192,128]{3,2,1,0:T(8,128)} %param.4), channel_id=1, source_target_pairs={{8,0},{16,8},{24,16},{32,24},{40,32},{48,40},{56,48},{64,56},{72,6... | collective-permute-start | bytes 1769480 | tf_op jit(solution)/shard_map/ppermute | solution.py:23
  17.6 3.6 %collective-permute-start.1 = (f32[3,2,2,128]{3,2,1,0:T(2,128)S(1)}, f32[3,2,2,128]{3,2,1,0:T(2,128)S(1)}, u32[]{:S(2)}, u32[]{:S(2)}) collective-permute-start(f32[3,2,2,128]{3,2,1,0:T(2,128)S(1)} %get-tuple-element.146), channel_id=1, source_target_pairs={{0,1},{1,2},{2,3},{3,4},{4,5},{5,6},{6,7},{8,9},{9,10},{10,11},{11... | collective-permute-start | bytes 18440 | tf_op jit(solution)/shard_map/ppermute | solution.py:21
  28.6 23.4 %all_gather.3 = f32[3,4,8]{1,0,2:T(4,128)S(1)} all-gather(f32[3,4,1]{1,0,2:T(4,128)S(1)} %maximum_bitcast_fusion.9), channel_id=1, replica_groups=mesh['gx'=64,'gy'=8] {'gy'}, dimensions={2}, use_global_device_ids=true | all-gather | bytes 432 | tf_op jit(solution)/shard_map/all_gather | solution.py:86
  54.3 2.7 %fusion.61 = f32[3,2,192,128]{3,2,1,0:T(8,128)S(1)} fusion(f32[3,2,194,128]{3,2,1,0:T(8,128)S(1)} %constant_dynamic-update-slice_fusion, f32[3,2,192,128]{3,2,1,0:T(8,128)S(1)} %copy-done, f32[3,2,2,128]{3,2,1,0:T(2,128)S(1)} %copy-done.12, f32[3,2,192,128]{3,2,1,0:T(8,128)} %collective-permute-done.3, f32[3,2,192,128]{3,2,1,0:T(8,128)} %collective-permute-done.2, ...), kind=kLoop, calls=%fused_computation.79 | loop fusion | flops 7077888 | bytes 7084032 | tf_op jit(solution)/shard_map/add | solution.py:117
  59.7 5.2 %all-to-all-start = ((f32[2,8,96]{2,0,1:T(2,128)}), f32[2,8,96]{2,0,1:T(2,128)S(1)}, u32[]{:S(2)}, u32[]{:S(2)}) async-start(f32[2,8,96]{2,0,1:T(2,128)} %pad_maximum_fusion.11), calls=%async_computation | async-start | bytes 16384 | tf_op jit(solution)/shard_map/all_to_all | solution.py:129
  83.8 7.7 %fusion.235 = (f32[1,96]{1,0:T(1,128)S(1)}, f32[1,96]{1,0:T(1,128)S(1)}, f32[1,96]{1,0:T(1,128)S(1)}, f32[1,96]{1,0:T(1,128)S(1)}, f32[1,96]{1,0:T(1,128)S(1)}, ...) fusion(f32[2,8,96]{2,0,1:T(2,128)S(1)} %all-to-all-done, ...), kind=kLoop, calls=%fused_computation.345 | loop fusion | flops 4512 | bytes 10476 | tf_op jit(solution)/shard_map/add | solution.py:48
  92.9 7.2 %all-to-all-start.1 = ((f32[2,8,96]{2,0,1:T(2,128)}), f32[2,8,96]{2,0,1:T(2,128)S(1)}, u32[]{:S(2)}, u32[]{:S(2)}) async-start(f32[2,8,96]{2,0,1:T(2,128)} %copy.10), calls=%async_computation.1 | async-start | bytes 16384 | tf_op jit(solution)/shard_map/all_to_all | solution.py:133
  100.8 5.6 %all-to-all-done.1 = f32[2,8,96]{2,0,1:T(2,128)S(1)} async-done(((f32[2,8,96]{2,0,1:T(2,128)}), f32[2,8,96]{2,0,1:T(2,128)S(1)}, u32[]{:S(2)}, u32[]{:S(2)}) %all-to-all-start.1) | async-done | bytes 6176 | tf_op jit(solution)/shard_map/all_to_all | solution.py:133
  109.4 2.4 collective-permute-start.6
  112.5 3.3 %collective-permute-start.4 = (f32[3,2,2,128]{3,2,1,0:T(2,128)S(1)}, f32[3,2,2,128]{3,2,1,0:T(2,128)S(1)}, u32[]{:S(2)}, u32[]{:S(2)}) collective-permute-start(f32[3,2,2,128]{3,2,1,0:T(2,128)S(1)} %get-tuple-element.129), channel_id=1, source_target_pairs={{1,0},{2,1},{3,2},{4,3},{5,4},{6,5},{7,6},{9,8},{10,9},{11,10},{12... | collective-permute-start | bytes 18440 | tf_op jit(solution)/shard_map/ppermute | solution.py:23
  115.8 2.5 %collective-permute-start.5 = (f32[3,2,2,128]{3,2,1,0:T(2,128)S(1)}, f32[3,2,2,128]{3,2,1,0:T(2,128)S(1)}, u32[]{:S(2)}, u32[]{:S(2)}) collective-permute-start(f32[3,2,2,128]{3,2,1,0:T(2,128)S(1)} %get-tuple-element.128), channel_id=1, source_target_pairs={{0,1},{1,2},{2,3},{3,4},{4,5},{5,6},{6,7},{8,9},{9,10},{10,11},{11... | collective-permute-start | bytes 18440 | tf_op jit(solution)/shard_map/ppermute | solution.py:21
  118.6 2.7 %collective-permute-done.5 = f32[3,2,2,128]{3,2,1,0:T(2,128)S(1)} collective-permute-done((f32[3,2,2,128]{3,2,1,0:T(2,128)S(1)}, f32[3,2,2,128]{3,2,1,0:T(2,128)S(1)}, u32[]{:S(2)}, u32[]{:S(2)}) %collective-permute-start.5) | collective-permute-done | bytes 6176 | tf_op jit(solution)/shard_map/ppermute | solution.py:21
  121.3 2.5 %collective-permute-done.6 = f32[3,2,192,128]{3,2,1,0:T(8,128)S(1)} collective-permute-done((f32[3,2,192,128]{3,2,1,0:T(8,128)S(1)}, f32[3,2,192,128]{3,2,1,0:T(8,128)S(1)}, u32[]{:S(2)}, u32[]{:S(2)}) %collective-permute-start.6) | collective-permute-done | bytes 589856 | tf_op jit(solution)/shard_map/ppermute | solution.py:21
  127.0 4.7 %all-to-all-start.2 = ((f32[2,8,96]{2,0,1:T(2,128)}), f32[2,8,96]{2,0,1:T(2,128)S(1)}, u32[]{:S(2)}, u32[]{:S(2)}) async-start(f32[2,8,96]{2,0,1:T(2,128)} %pad_maximum_fusion.13), calls=%async_computation.2 | async-start | bytes 16384 | tf_op jit(solution)/shard_map/all_to_all | solution.py:129
  150.5 7.5 %fusion.206 = (f32[1,96]{1,0:T(1,128)S(1)}, f32[1,96]{1,0:T(1,128)S(1)}, f32[1,96]{1,0:T(1,128)S(1)}, f32[1,96]{1,0:T(1,128)S(1)}, f32[1,96]{1,0:T(1,128)S(1)}, ...) fusion(f32[2,8,96]{2,0,1:T(2,128)S(1)} %all-to-all-done.2, ...), kind=kLoop, calls=%fused_computation.301 | loop fusion | flops 4512 | bytes 10476 | tf_op jit(solution)/shard_map/add | solution.py:48
  158.8 13.3 %all_to_all.30 = f32[2,8,96]{2,0,1:T(2,128)S(1)} all-to-all(f32[2,8,96]{2,0,1:T(2,128)S(1)} %copy.13), channel_id=1, replica_groups=mesh['gx'=64,'gy'=8] {'gy'}, dimensions={1} | all-to-all | bytes 12288 | tf_op jit(solution)/shard_map/all_to_all | solution.py:133
  175.1 2.4 collective-permute-start.10
  178.2 3.3 %collective-permute-start.8 = (f32[3,2,2,128]{3,2,1,0:T(2,128)S(1)}, f32[3,2,2,128]{3,2,1,0:T(2,128)S(1)}, u32[]{:S(2)}, u32[]{:S(2)}) collective-permute-start(f32[3,2,2,128]{3,2,1,0:T(2,128)S(1)} %get-tuple-element.113), channel_id=1, source_target_pairs={{1,0},{2,1},{3,2},{4,3},{5,4},{6,5},{7,6},{9,8},{10,9},{11,10},{12... | collective-permute-start | bytes 18440 | tf_op jit(solution)/shard_map/ppermute | solution.py:23
  181.5 2.7 %collective-permute-start.9 = (f32[3,2,2,128]{3,2,1,0:T(2,128)S(1)}, f32[3,2,2,128]{3,2,1,0:T(2,128)S(1)}, u32[]{:S(2)}, u32[]{:S(2)}) collective-permute-start(f32[3,2,2,128]{3,2,1,0:T(2,128)S(1)} %get-tuple-element.112), channel_id=1, source_target_pairs={{0,1},{1,2},{2,3},{3,4},{4,5},{5,6},{6,7},{8,9},{9,10},{10,11},{11... | collective-permute-start | bytes 18440 | tf_op jit(solution)/shard_map/ppermute | solution.py:21
  184.6 2.5 %collective-permute-done.9 = f32[3,2,2,128]{3,2,1,0:T(2,128)S(1)} collective-permute-done((f32[3,2,2,128]{3,2,1,0:T(2,128)S(1)}, f32[3,2,2,128]{3,2,1,0:T(2,128)S(1)}, u32[]{:S(2)}, u32[]{:S(2)}) %collective-permute-start.9) | collective-permute-done | bytes 6176 | tf_op jit(solution)/shard_map/ppermute | solution.py:21
  187.1 2.5 %collective-permute-done.10 = f32[3,2,192,128]{3,2,1,0:T(8,128)S(1)} collective-permute-done((f32[3,2,192,128]{3,2,1,0:T(8,128)S(1)}, f32[3,2,192,128]{3,2,1,0:T(8,128)S(1)}, u32[]{:S(2)}, u32[]{:S(2)}) %collective-permute-start.10) | collective-permute-done | bytes 589856 | tf_op jit(solution)/shard_map/ppermute | solution.py:21
  192.7 4.7 %all-to-all-start.4 = ((f32[2,8,96]{2,0,1:T(2,128)}), f32[2,8,96]{2,0,1:T(2,128)S(1)}, u32[]{:S(2)}, u32[]{:S(2)}) async-start(f32[2,8,96]{2,0,1:T(2,128)} %pad_maximum_fusion.15), calls=%async_computation.4 | async-start | bytes 16384 | tf_op jit(solution)/shard_map/all_to_all | solution.py:129
  216.3 7.6 %fusion.177 = (f32[1,96]{1,0:T(1,128)S(1)}, f32[1,96]{1,0:T(1,128)S(1)}, f32[1,96]{1,0:T(1,128)S(1)}, f32[1,96]{1,0:T(1,128)S(1)}, f32[1,96]{1,0:T(1,128)S(1)}, ...) fusion(f32[2,8,96]{2,0,1:T(2,128)S(1)} %all-to-all-done.4, ...), kind=kLoop, calls=%fused_computation.257 | loop fusion | flops 4512 | bytes 10476 | tf_op jit(solution)/shard_map/add | solution.py:48
  225.3 13.3 %all_to_all.31 = f32[2,8,96]{2,0,1:T(2,128)S(1)} all-to-all(f32[2,8,96]{2,0,1:T(2,128)S(1)} %copy.16), channel_id=1, replica_groups=mesh['gx'=64,'gy'=8] {'gy'}, dimensions={1} | all-to-all | bytes 12288 | tf_op jit(solution)/shard_map/all_to_all | solution.py:133
  (153 shorter events, 39.4 us)
Async XLA Ops:
  0.0 53.1 %collective-permute-start.3 = (f32[3,2,192,128]{3,2,1,0:T(8,128)}, f32[3,2,192,128]{3,2,1,0:T(8,128)}, u32[]{:S(2)}, u32[]{:S(2)}) collective-permute-start(f32[3,2,192,128]{3,2,1,0:T(8,128)} %param.4), channel_id=1, source_target_pairs={{8,0},{16,8},{24,16},{32,24},{40,32},{48,40},{56,48},{64,56},{72,6... | collective-permute-start | bytes 1769480 | tf_op jit(solution)/shard_map/ppermute | solution.py:23
  12.6 40.5 %collective-permute-start.2 = (f32[3,2,192,128]{3,2,1,0:T(8,128)}, f32[3,2,192,128]{3,2,1,0:T(8,128)}, u32[]{:S(2)}, u32[]{:S(2)}) collective-permute-start(f32[3,2,192,128]{3,2,1,0:T(8,128)} %param.4), channel_id=1, source_target_pairs={{0,8},{8,16},{16,24},{24,32},{32,40},{40,48},{48,56},{56,64},{64,7... | collective-permute-start | bytes 1769480 | tf_op jit(solution)/shard_map/ppermute | solution.py:21
  15.3 37.7 %collective-permute-start = (f32[3,2,2,128]{3,2,1,0:T(2,128)S(1)}, f32[3,2,2,128]{3,2,1,0:T(2,128)S(1)}, u32[]{:S(2)}, u32[]{:S(2)}) collective-permute-start(f32[3,2,2,128]{3,2,1,0:T(2,128)S(1)} %get-tuple-element.147), channel_id=1, source_target_pairs={{1,0},{2,1},{3,2},{4,3},{5,4},{6,5},{7,6},{9,8},{10,9},{11,10},{12... | collective-permute-start | bytes 18440 | tf_op jit(solution)/shard_map/ppermute | solution.py:23
  17.6 5.2 %copy-start = (f32[3,2,192,128]{3,2,1,0:T(8,128)S(1)}, f32[3,2,192,128]{3,2,1,0:T(8,128)}, u32[]{:S(2)}) copy-start(f32[3,2,192,128]{3,2,1,0:T(8,128)} %param.4) | copy-start | bytes 1769476
  17.6 35.4 %collective-permute-start.1 = (f32[3,2,2,128]{3,2,1,0:T(2,128)S(1)}, f32[3,2,2,128]{3,2,1,0:T(2,128)S(1)}, u32[]{:S(2)}, u32[]{:S(2)}) collective-permute-start(f32[3,2,2,128]{3,2,1,0:T(2,128)S(1)} %get-tuple-element.146), channel_id=1, source_target_pairs={{0,1},{1,2},{2,3},{3,4},{4,5},{5,6},{6,7},{8,9},{9,10},{10,11},{11... | collective-permute-start | bytes 18440 | tf_op jit(solution)/shard_map/ppermute | solution.py:21
  24.2 1.7 copy-start.3
  52.0 1.7 copy-start.1
  52.0 1.6 copy-start.2
  52.0 1.6 copy-start.5
  59.7 24.0 %all-to-all-start = ((f32[2,8,96]{2,0,1:T(2,128)}), f32[2,8,96]{2,0,1:T(2,128)S(1)}, u32[]{:S(2)}, u32[]{:S(2)}) async-start(f32[2,8,96]{2,0,1:T(2,128)} %pad_maximum_fusion.11), calls=%async_computation | async-start | bytes 16384 | tf_op jit(solution)/shard_map/all_to_all | solution.py:129
  92.2 14.4 %copy-start.19 = (f32[1,192]{1,0:T(1,128)S(1)}, f32[1,192]{1,0:T(1,128)}, u32[]{:S(2)}) copy-start(f32[1,192]{1,0:T(1,128)} %get-tuple-element.237) | copy-start | bytes 2308
  92.2 66.5 %copy-start.13 = (f32[1,96]{1,0:T(1,128)}, f32[1,96]{1,0:T(1,128)S(1)}, u32[]{:S(2)}) copy-start(f32[1,96]{1,0:T(1,128)S(1)} %broadcast.6105) | copy-start | bytes 1156
  92.9 13.5 %all-to-all-start.1 = ((f32[2,8,96]{2,0,1:T(2,128)}), f32[2,8,96]{2,0,1:T(2,128)S(1)}, u32[]{:S(2)}, u32[]{:S(2)}) async-start(f32[2,8,96]{2,0,1:T(2,128)} %copy.10), calls=%async_computation.1 | async-start | bytes 16384 | tf_op jit(solution)/shard_map/all_to_all | solution.py:133
  107.4 13.9 %collective-permute-start.7 = (f32[3,2,192,128]{3,2,1,0:T(8,128)S(1)}, f32[3,2,192,128]{3,2,1,0:T(8,128)S(1)}, u32[]{:S(2)}, u32[]{:S(2)}) collective-permute-start(f32[3,2,192,128]{3,2,1,0:T(8,128)S(1)} %multiply_subtract_fusion.6), channel_id=1, source_target_pairs={{8,0},{16,8},{24,16},{32,24},{40,32},{48,40},{56,48},{64,56},{72,6... | collective-permute-start | bytes 1769480 | tf_op jit(solution)/shard_map/ppermute | solution.py:23
  109.4 14.5 %collective-permute-start.6 = (f32[3,2,192,128]{3,2,1,0:T(8,128)S(1)}, f32[3,2,192,128]{3,2,1,0:T(8,128)S(1)}, u32[]{:S(2)}, u32[]{:S(2)}) collective-permute-start(f32[3,2,192,128]{3,2,1,0:T(8,128)S(1)} %multiply_subtract_fusion.6), channel_id=1, source_target_pairs={{0,8},{8,16},{16,24},{24,32},{32,40},{40,48},{48,56},{56,64},{64,7... | collective-permute-start | bytes 1769480 | tf_op jit(solution)/shard_map/ppermute | solution.py:21
  112.5 6.2 %collective-permute-start.4 = (f32[3,2,2,128]{3,2,1,0:T(2,128)S(1)}, f32[3,2,2,128]{3,2,1,0:T(2,128)S(1)}, u32[]{:S(2)}, u32[]{:S(2)}) collective-permute-start(f32[3,2,2,128]{3,2,1,0:T(2,128)S(1)} %get-tuple-element.129), channel_id=1, source_target_pairs={{1,0},{2,1},{3,2},{4,3},{5,4},{6,5},{7,6},{9,8},{10,9},{11,10},{12... | collective-permute-start | bytes 18440 | tf_op jit(solution)/shard_map/ppermute | solution.py:23
  115.8 5.5 %collective-permute-start.5 = (f32[3,2,2,128]{3,2,1,0:T(2,128)S(1)}, f32[3,2,2,128]{3,2,1,0:T(2,128)S(1)}, u32[]{:S(2)}, u32[]{:S(2)}) collective-permute-start(f32[3,2,2,128]{3,2,1,0:T(2,128)S(1)} %get-tuple-element.128), channel_id=1, source_target_pairs={{0,1},{1,2},{2,3},{3,4},{4,5},{5,6},{6,7},{8,9},{9,10},{10,11},{11... | collective-permute-start | bytes 18440 | tf_op jit(solution)/shard_map/ppermute | solution.py:21
  127.0 23.5 %all-to-all-start.2 = ((f32[2,8,96]{2,0,1:T(2,128)}), f32[2,8,96]{2,0,1:T(2,128)S(1)}, u32[]{:S(2)}, u32[]{:S(2)}) async-start(f32[2,8,96]{2,0,1:T(2,128)} %pad_maximum_fusion.13), calls=%async_computation.2 | async-start | bytes 16384 | tf_op jit(solution)/shard_map/all_to_all | solution.py:129
  133.7 38.6 %copy-start.17 = (f32[1,192]{1,0:T(1,128)S(1)}, f32[1,192]{1,0:T(1,128)}, u32[]{:S(2)}) copy-start(f32[1,192]{1,0:T(1,128)} %get-tuple-element.236) | copy-start | bytes 2308
  173.2 13.9 %collective-permute-start.11 = (f32[3,2,192,128]{3,2,1,0:T(8,128)S(1)}, f32[3,2,192,128]{3,2,1,0:T(8,128)S(1)}, u32[]{:S(2)}, u32[]{:S(2)}) collective-permute-start(f32[3,2,192,128]{3,2,1,0:T(8,128)S(1)} %multiply_subtract_fusion.5), channel_id=1, source_target_pairs={{8,0},{16,8},{24,16},{32,24},{40,32},{48,40},{56,48},{64,56},{72,6... | collective-permute-start | bytes 1769480 | tf_op jit(solution)/shard_map/ppermute | solution.py:23
  175.1 14.5 %collective-permute-start.10 = (f32[3,2,192,128]{3,2,1,0:T(8,128)S(1)}, f32[3,2,192,128]{3,2,1,0:T(8,128)S(1)}, u32[]{:S(2)}, u32[]{:S(2)}) collective-permute-start(f32[3,2,192,128]{3,2,1,0:T(8,128)S(1)} %multiply_subtract_fusion.5), channel_id=1, source_target_pairs={{0,8},{8,16},{16,24},{24,32},{32,40},{40,48},{48,56},{56,64},{64,7... | collective-permute-start | bytes 1769480 | tf_op jit(solution)/shard_map/ppermute | solution.py:21
  178.2 6.4 %collective-permute-start.8 = (f32[3,2,2,128]{3,2,1,0:T(2,128)S(1)}, f32[3,2,2,128]{3,2,1,0:T(2,128)S(1)}, u32[]{:S(2)}, u32[]{:S(2)}) collective-permute-start(f32[3,2,2,128]{3,2,1,0:T(2,128)S(1)} %get-tuple-element.113), channel_id=1, source_target_pairs={{1,0},{2,1},{3,2},{4,3},{5,4},{6,5},{7,6},{9,8},{10,9},{11,10},{12... | collective-permute-start | bytes 18440 | tf_op jit(solution)/shard_map/ppermute | solution.py:23
  181.5 5.5 %collective-permute-start.9 = (f32[3,2,2,128]{3,2,1,0:T(2,128)S(1)}, f32[3,2,2,128]{3,2,1,0:T(2,128)S(1)}, u32[]{:S(2)}, u32[]{:S(2)}) collective-permute-start(f32[3,2,2,128]{3,2,1,0:T(2,128)S(1)} %get-tuple-element.112), channel_id=1, source_target_pairs={{0,1},{1,2},{2,3},{3,4},{4,5},{5,6},{6,7},{8,9},{9,10},{10,11},{11... | collective-permute-start | bytes 18440 | tf_op jit(solution)/shard_map/ppermute | solution.py:21
  192.7 23.6 %all-to-all-start.4 = ((f32[2,8,96]{2,0,1:T(2,128)}), f32[2,8,96]{2,0,1:T(2,128)S(1)}, u32[]{:S(2)}, u32[]{:S(2)}) async-start(f32[2,8,96]{2,0,1:T(2,128)} %pad_maximum_fusion.15), calls=%async_computation.4 | async-start | bytes 16384 | tf_op jit(solution)/shard_map/all_to_all | solution.py:129
  (13 other events, 14.1 us)
where the time goes:
time: 243 us; the launch traced here: 241 us
  starting transfers between devices  62.7 us (26%)
  between operations  55.7 us (23%)
  blocking collectives  50 us (21%)
  other arithmetic  34.1 us (14%)
  local copies, waits for them, and re-layouts  17.6 us (7%)
  waiting for transfers between devices  15.9 us (7%)
  matrix products  5.06 us (2%)
    all_to_all x2, blocking collectives, body(): lax.all_to_all(jnp.stack([lower_prev, upper_next]), 'gy', split_axis=1, c...  26.6 us
    ppermute x6, starting transfers between devices, with_halo(): lax.ppermute(head, axis, [((i + 1) % count, i) for i in range(ends)])  25.5 us
    all_gather x1, blocking collectives, body(): every_tip = lax.all_gather(own_tips, 'gy', axis=2, tiled=True)  23.4 us
    add x3, other arithmetic, reduced(): back = last_vals[block] - tail_v * prev_last + tail_v * prev_q * front  22.8 us
    ppermute x6, starting transfers between devices, with_halo(): lax.ppermute(tail, axis, [(i, (i + 1) % count) for i in range(ends)])  15.5 us
    all_to_all x3, starting transfers between devices, body(): lax.all_to_all(edges.reshape(2, blocks, -1), 'gy', split_axis=1, concat_a...  14.6 us
    ppermute x6, waiting for transfers between devices, with_halo(): lax.ppermute(tail, axis, [(i, (i + 1) % count) for i in range(ends)])  10.3 us
    all_to_all x1, starting transfers between devices, body(): lax.all_to_all(jnp.stack([lower_prev, upper_next]), 'gy', split_axis=1, c...  7.21 us
  transfers between devices with their start and end apart: 16, of which 5 were waited for; matrix products, arithmetic and copies ran while one was open for 5% of the time, Pallas kernels for 0%

commit v1 on v0

--- a/solution.py
+++ b/solution.py
@@ -8,6 +8,13 @@
 new_weight = (8.0 / 15.0, 5.0 / 12.0, 3.0 / 4.0)
 old_weight = (0.0, -17.0 / 60.0, -5.0 / 12.0)
 courant = (0.3, 0.2, 0.3)
+
+
+def trade_parts(x, axis, split, join):
+    size = lax.axis_size(axis)
+    blocks = jnp.stack(jnp.split(x, size, axis=split), axis=0)
+    blocks = lax.all_to_all(blocks, axis, split_axis=0, concat_axis=0)
+    return jnp.concatenate(blocks, axis=join)
 
 
 def with_halo(cells, sides, width, closed):
@@ -130,9 +137,7 @@
             edges.reshape(2, blocks, -1), "gy", split_axis=1, concat_axis=1, tiled=True
         )
         lower_prev, upper_next = reduced(grouped[0], grouped[1], tips)
-        returned = lax.all_to_all(
-            jnp.stack([lower_prev, upper_next]), "gy", split_axis=1, concat_axis=1, tiled=True
-        ).reshape(2, -1)
+        returned = trade_parts(jnp.stack([lower_prev, upper_next]), "gy", 1, 1).reshape(2, -1)
         lower_own = returned[0]
         upper_own = returned[1]
         lower_own = lower_own.reshape(3, planes, spans)[:, :, None, :]

time: 243 us -> 247 us (1.016)
  local copies, waits for them, and re-layouts: 17.6 us -> 21.6 us
    unnamed x44 -> x65, local copies, waits for them, and re-layouts: 4.78 us -> 8.82 us
where the time goes in v1:
time: 247 us; the launch traced here: 245 us
  starting transfers between devices  62.7 us (25%)
  between operations  55.5 us (22%)
  blocking collectives  50 us (20%)
  other arithmetic  34 us (14%)
  local copies, waits for them, and re-layouts  21.6 us (9%)
  waiting for transfers between devices  15.9 us (6%)
  matrix products  5.06 us (2%)
    all_to_all x2, blocking collectives, trade_parts(): blocks = lax.all_to_all(blocks, axis, split_axis=0, concat_axis=0)  26.6 us
    ppermute x6, starting transfers between devices, with_halo(): lax.ppermute(head, axis, [((i + 1) % count, i) for i in range(ends)])  25.5 us
    all_gather x1, blocking collectives, body(): every_tip = lax.all_gather(own_tips, 'gy', axis=2, tiled=True)  23.4 us
    add x3, other arithmetic, reduced(): back = last_vals[block] - tail_v * prev_last + tail_v * prev_q * front  22.6 us
    ppermute x6, starting transfers between devices, with_halo(): lax.ppermute(tail, axis, [(i, (i + 1) % count) for i in range(ends)])  15.5 us
    all_to_all x3, starting transfers between devices, body(): lax.all_to_all(edges.reshape(2, blocks, -1), 'gy', split_axis=1, concat_a...  14.6 us
    ppermute x6, waiting for transfers between devices, with_halo(): lax.ppermute(tail, axis, [(i, (i + 1) % count) for i in range(ends)])  10.3 us
    unnamed x65, local copies, waits for them, and re-layouts  8.82 us
  transfers between devices with their start and end apart: 16, of which 5 were waited for; matrix products, arithmetic and copies ran while one was open for 5% of the time, Pallas kernels for 0%

profile of v1, /device:TPU:8, one launch (start us, length us, event | category | flops | bytes accessed | tf_op | source)
XLA Modules:
  0.0 244.8 jit_solution(14800359754178931780)
XLA Ops:
  0.0 12.6 %collective-permute-start.3 = (f32[3,2,192,128]{3,2,1,0:T(8,128)}, f32[3,2,192,128]{3,2,1,0:T(8,128)}, u32[]{:S(2)}, u32[]{:S(2)}) collective-permute-start(f32[3,2,192,128]{3,2,1,0:T(8,128)} %param.4), channel_id=1, source_target_pairs={{8,0},{16,8},{24,16},{32,24},{40,32},{48,40},{56,48},{64,56},{72,6... | collective-permute-start | bytes 1769480 | tf_op jit(solution)/shard_map/ppermute | solution.py:30
  17.6 3.6 %collective-permute-start.1 = (f32[3,2,2,128]{3,2,1,0:T(2,128)S(1)}, f32[3,2,2,128]{3,2,1,0:T(2,128)S(1)}, u32[]{:S(2)}, u32[]{:S(2)}) collective-permute-start(f32[3,2,2,128]{3,2,1,0:T(2,128)S(1)} %get-tuple-element.146), channel_id=1, source_target_pairs={{0,1},{1,2},{2,3},{3,4},{4,5},{5,6},{6,7},{8,9},{9,10},{10,11},{11... | collective-permute-start | bytes 18440 | tf_op jit(solution)/shard_map/ppermute | solution.py:28
  28.6 23.4 %all_gather.3 = f32[3,4,8]{1,0,2:T(4,128)S(1)} all-gather(f32[3,4,1]{1,0,2:T(4,128)S(1)} %maximum_bitcast_fusion.9), channel_id=1, replica_groups=mesh['gx'=64,'gy'=8] {'gy'}, dimensions={2}, use_global_device_ids=true | all-gather | bytes 432 | tf_op jit(solution)/shard_map/all_gather | solution.py:93
  54.3 2.7 %fusion.61 = f32[3,2,192,128]{3,2,1,0:T(8,128)S(1)} fusion(f32[3,2,194,128]{3,2,1,0:T(8,128)S(1)} %constant_dynamic-update-slice_fusion, f32[3,2,192,128]{3,2,1,0:T(8,128)S(1)} %copy-done, f32[3,2,2,128]{3,2,1,0:T(2,128)S(1)} %copy-done.12, f32[3,2,192,128]{3,2,1,0:T(8,128)} %collective-permute-done.3, f32[3,2,192,128]{3,2,1,0:T(8,128)} %collective-permute-done.2, ...), kind=kLoop, calls=%fused_computation.79 | loop fusion | flops 7077888 | bytes 7084032 | tf_op jit(solution)/shard_map/add | solution.py:124
  59.7 5.2 %all-to-all-start = ((f32[2,8,96]{2,0,1:T(2,128)}), f32[2,8,96]{2,0,1:T(2,128)S(1)}, u32[]{:S(2)}, u32[]{:S(2)}) async-start(f32[2,8,96]{2,0,1:T(2,128)} %pad_maximum_fusion.11), calls=%async_computation | async-start | bytes 16384 | tf_op jit(solution)/shard_map/all_to_all | solution.py:136
  83.5 7.5 %fusion.256 = (f32[1,96]{1,0:T(1,128)S(1)}, f32[1,96]{1,0:T(1,128)S(1)}, f32[1,96]{1,0:T(1,128)S(1)}, f32[1,96]{1,0:T(1,128)S(1)}, f32[1,96]{1,0:T(1,128)S(1)}, ...) fusion(f32[2,8,96]{2,0,1:T(2,128)S(1)} %all-to-all-done, ...), kind=kLoop, calls=%fused_computation.432 | loop fusion | flops 4512 | bytes 10476 | tf_op jit(solution)/shard_map/add | solution.py:55
  96.3 7.2 %all-to-all-start.1 = ((f32[8,2,1,96]{3,1,2,0:T(2,128)}), f32[8,2,1,96]{3,1,2,0:T(2,128)S(1)}, u32[]{:S(2)}, u32[]{:S(2)}) async-start(f32[8,2,1,96]{3,1,2,0:T(2,128)} %constant_dynamic-update-slice_fusion.2), calls=%async_computation.1 | async-start | bytes 16384 | tf_op jit(solution)/shard_map/all_to_all | solution.py:16
  104.2 5.6 %all-to-all-done.1 = f32[8,2,1,96]{3,1,2,0:T(2,128)S(1)} async-done(((f32[8,2,1,96]{3,1,2,0:T(2,128)}), f32[8,2,1,96]{3,1,2,0:T(2,128)S(1)}, u32[]{:S(2)}, u32[]{:S(2)}) %all-to-all-start.1) | async-done | bytes 6176 | tf_op jit(solution)/shard_map/all_to_all | solution.py:16
  112.7 2.4 collective-permute-start.6
  115.8 3.3 %collective-permute-start.4 = (f32[3,2,2,128]{3,2,1,0:T(2,128)S(1)}, f32[3,2,2,128]{3,2,1,0:T(2,128)S(1)}, u32[]{:S(2)}, u32[]{:S(2)}) collective-permute-start(f32[3,2,2,128]{3,2,1,0:T(2,128)S(1)} %get-tuple-element.129), channel_id=1, source_target_pairs={{1,0},{2,1},{3,2},{4,3},{5,4},{6,5},{7,6},{9,8},{10,9},{11,10},{12... | collective-permute-start | bytes 18440 | tf_op jit(solution)/shard_map/ppermute | solution.py:30
  119.2 2.5 %collective-permute-start.5 = (f32[3,2,2,128]{3,2,1,0:T(2,128)S(1)}, f32[3,2,2,128]{3,2,1,0:T(2,128)S(1)}, u32[]{:S(2)}, u32[]{:S(2)}) collective-permute-start(f32[3,2,2,128]{3,2,1,0:T(2,128)S(1)} %get-tuple-element.128), channel_id=1, source_target_pairs={{0,1},{1,2},{2,3},{3,4},{4,5},{5,6},{6,7},{8,9},{9,10},{10,11},{11... | collective-permute-start | bytes 18440 | tf_op jit(solution)/shard_map/ppermute | solution.py:28
  122.0 2.7 %collective-permute-done.5 = f32[3,2,2,128]{3,2,1,0:T(2,128)S(1)} collective-permute-done((f32[3,2,2,128]{3,2,1,0:T(2,128)S(1)}, f32[3,2,2,128]{3,2,1,0:T(2,128)S(1)}, u32[]{:S(2)}, u32[]{:S(2)}) %collective-permute-start.5) | collective-permute-done | bytes 6176 | tf_op jit(solution)/shard_map/ppermute | solution.py:28
  124.7 2.5 %collective-permute-done.6 = f32[3,2,192,128]{3,2,1,0:T(8,128)S(1)} collective-permute-done((f32[3,2,192,128]{3,2,1,0:T(8,128)S(1)}, f32[3,2,192,128]{3,2,1,0:T(8,128)S(1)}, u32[]{:S(2)}, u32[]{:S(2)}) %collective-permute-start.6) | collective-permute-done | bytes 589856 | tf_op jit(solution)/shard_map/ppermute | solution.py:28
  130.4 4.7 %all-to-all-start.2 = ((f32[2,8,96]{2,0,1:T(2,128)}), f32[2,8,96]{2,0,1:T(2,128)S(1)}, u32[]{:S(2)}, u32[]{:S(2)}) async-start(f32[2,8,96]{2,0,1:T(2,128)} %pad_maximum_fusion.12), calls=%async_computation.2 | async-start | bytes 16384 | tf_op jit(solution)/shard_map/all_to_all | solution.py:136
  154.0 7.6 %fusion.227 = (f32[1,96]{1,0:T(1,128)S(1)}, f32[1,96]{1,0:T(1,128)S(1)}, f32[1,96]{1,0:T(1,128)S(1)}, f32[1,96]{1,0:T(1,128)S(1)}, f32[1,96]{1,0:T(1,128)S(1)}, ...) fusion(f32[2,8,96]{2,0,1:T(2,128)S(1)} %all-to-all-done.2, ...), kind=kLoop, calls=%fused_computation.388 | loop fusion | flops 4512 | bytes 10476 | tf_op jit(solution)/shard_map/add | solution.py:55
  162.6 13.3 %all_to_all.30 = f32[8,2,1,96]{3,1,2,0:T(2,128)S(1)} all-to-all(f32[8,2,1,96]{3,1,2,0:T(2,128)S(1)} %constant_dynamic-update-slice_fusion.10), channel_id=1, replica_groups=mesh['gx'=64,'gy'=8] {'gy'}, dimensions={0} | all-to-all | bytes 12288 | tf_op jit(solution)/shard_map/all_to_all | solution.py:16
  178.9 2.4 collective-permute-start.10
  182.0 3.3 %collective-permute-start.8 = (f32[3,2,2,128]{3,2,1,0:T(2,128)S(1)}, f32[3,2,2,128]{3,2,1,0:T(2,128)S(1)}, u32[]{:S(2)}, u32[]{:S(2)}) collective-permute-start(f32[3,2,2,128]{3,2,1,0:T(2,128)S(1)} %get-tuple-element.113), channel_id=1, source_target_pairs={{1,0},{2,1},{3,2},{4,3},{5,4},{6,5},{7,6},{9,8},{10,9},{11,10},{12... | collective-permute-start | bytes 18440 | tf_op jit(solution)/shard_map/ppermute | solution.py:30
  185.3 2.7 %collective-permute-start.9 = (f32[3,2,2,128]{3,2,1,0:T(2,128)S(1)}, f32[3,2,2,128]{3,2,1,0:T(2,128)S(1)}, u32[]{:S(2)}, u32[]{:S(2)}) collective-permute-start(f32[3,2,2,128]{3,2,1,0:T(2,128)S(1)} %get-tuple-element.112), channel_id=1, source_target_pairs={{0,1},{1,2},{2,3},{3,4},{4,5},{5,6},{6,7},{8,9},{9,10},{10,11},{11... | collective-permute-start | bytes 18440 | tf_op jit(solution)/shard_map/ppermute | solution.py:28
  188.4 2.5 %collective-permute-done.9 = f32[3,2,2,128]{3,2,1,0:T(2,128)S(1)} collective-permute-done((f32[3,2,2,128]{3,2,1,0:T(2,128)S(1)}, f32[3,2,2,128]{3,2,1,0:T(2,128)S(1)}, u32[]{:S(2)}, u32[]{:S(2)}) %collective-permute-start.9) | collective-permute-done | bytes 6176 | tf_op jit(solution)/shard_map/ppermute | solution.py:28
  190.9 2.5 %collective-permute-done.10 = f32[3,2,192,128]{3,2,1,0:T(8,128)S(1)} collective-permute-done((f32[3,2,192,128]{3,2,1,0:T(8,128)S(1)}, f32[3,2,192,128]{3,2,1,0:T(8,128)S(1)}, u32[]{:S(2)}, u32[]{:S(2)}) %collective-permute-start.10) | collective-permute-done | bytes 589856 | tf_op jit(solution)/shard_map/ppermute | solution.py:28
  196.5 4.7 %all-to-all-start.4 = ((f32[2,8,96]{2,0,1:T(2,128)}), f32[2,8,96]{2,0,1:T(2,128)S(1)}, u32[]{:S(2)}, u32[]{:S(2)}) async-start(f32[2,8,96]{2,0,1:T(2,128)} %pad_maximum_fusion.13), calls=%async_computation.4 | async-start | bytes 16384 | tf_op jit(solution)/shard_map/all_to_all | solution.py:136
  219.9 7.5 %fusion.198 = (f32[1,96]{1,0:T(1,128)S(1)}, f32[1,96]{1,0:T(1,128)S(1)}, f32[1,96]{1,0:T(1,128)S(1)}, f32[1,96]{1,0:T(1,128)S(1)}, f32[1,96]{1,0:T(1,128)S(1)}, ...) fusion(f32[2,8,96]{2,0,1:T(2,128)S(1)} %all-to-all-done.4, ...), kind=kLoop, calls=%fused_computation.344 | loop fusion | flops 4512 | bytes 10476 | tf_op jit(solution)/shard_map/add | solution.py:55
  228.9 13.3 %all_to_all.31 = f32[8,2,1,96]{3,1,2,0:T(2,128)S(1)} all-to-all(f32[8,2,1,96]{3,1,2,0:T(2,128)S(1)} %constant_dynamic-update-slice_fusion.18), channel_id=1, replica_groups=mesh['gx'=64,'gy'=8] {'gy'}, dimensions={0} | all-to-all | bytes 12288 | tf_op jit(solution)/shard_map/all_to_all | solution.py:16
  (174 shorter events, 43.5 us)
Async XLA Ops:
  0.0 53.0 %collective-permute-start.3 = (f32[3,2,192,128]{3,2,1,0:T(8,128)}, f32[3,2,192,128]{3,2,1,0:T(8,128)}, u32[]{:S(2)}, u32[]{:S(2)}) collective-permute-start(f32[3,2,192,128]{3,2,1,0:T(8,128)} %param.4), channel_id=1, source_target_pairs={{8,0},{16,8},{24,16},{32,24},{40,32},{48,40},{56,48},{64,56},{72,6... | collective-permute-start | bytes 1769480 | tf_op jit(solution)/shard_map/ppermute | solution.py:30
  12.6 40.4 %collective-permute-start.2 = (f32[3,2,192,128]{3,2,1,0:T(8,128)}, f32[3,2,192,128]{3,2,1,0:T(8,128)}, u32[]{:S(2)}, u32[]{:S(2)}) collective-permute-start(f32[3,2,192,128]{3,2,1,0:T(8,128)} %param.4), channel_id=1, source_target_pairs={{0,8},{8,16},{16,24},{24,32},{32,40},{40,48},{48,56},{56,64},{64,7... | collective-permute-start | bytes 1769480 | tf_op jit(solution)/shard_map/ppermute | solution.py:28
  15.3 37.7 %collective-permute-start = (f32[3,2,2,128]{3,2,1,0:T(2,128)S(1)}, f32[3,2,2,128]{3,2,1,0:T(2,128)S(1)}, u32[]{:S(2)}, u32[]{:S(2)}) collective-permute-start(f32[3,2,2,128]{3,2,1,0:T(2,128)S(1)} %get-tuple-element.147), channel_id=1, source_target_pairs={{1,0},{2,1},{3,2},{4,3},{5,4},{6,5},{7,6},{9,8},{10,9},{11,10},{12... | collective-permute-start | bytes 18440 | tf_op jit(solution)/shard_map/ppermute | solution.py:30
  17.6 5.2 %copy-start = (f32[3,2,192,128]{3,2,1,0:T(8,128)S(1)}, f32[3,2,192,128]{3,2,1,0:T(8,128)}, u32[]{:S(2)}) copy-start(f32[3,2,192,128]{3,2,1,0:T(8,128)} %param.4) | copy-start | bytes 1769476
  17.6 35.4 %collective-permute-start.1 = (f32[3,2,2,128]{3,2,1,0:T(2,128)S(1)}, f32[3,2,2,128]{3,2,1,0:T(2,128)S(1)}, u32[]{:S(2)}, u32[]{:S(2)}) collective-permute-start(f32[3,2,2,128]{3,2,1,0:T(2,128)S(1)} %get-tuple-element.146), channel_id=1, source_target_pairs={{0,1},{1,2},{2,3},{3,4},{4,5},{5,6},{6,7},{8,9},{9,10},{10,11},{11... | collective-permute-start | bytes 18440 | tf_op jit(solution)/shard_map/ppermute | solution.py:28
  24.2 1.7 copy-start.3
  52.0 1.6 copy-start.1
  52.0 1.6 copy-start.2
  52.0 1.6 copy-start.5
  59.7 23.8 %all-to-all-start = ((f32[2,8,96]{2,0,1:T(2,128)}), f32[2,8,96]{2,0,1:T(2,128)S(1)}, u32[]{:S(2)}, u32[]{:S(2)}) async-start(f32[2,8,96]{2,0,1:T(2,128)} %pad_maximum_fusion.11), calls=%async_computation | async-start | bytes 16384 | tf_op jit(solution)/shard_map/all_to_all | solution.py:136
  91.7 70.8 %copy-start.13 = (f32[1,96]{1,0:T(1,128)}, f32[1,96]{1,0:T(1,128)S(1)}, u32[]{:S(2)}) copy-start(f32[1,96]{1,0:T(1,128)S(1)} %broadcast.6105) | copy-start | bytes 1156
  91.7 18.3 %copy-start.19 = (f32[1,192]{1,0:T(1,128)S(1)}, f32[1,192]{1,0:T(1,128)}, u32[]{:S(2)}) copy-start(f32[1,192]{1,0:T(1,128)} %get-tuple-element.261) | copy-start | bytes 2308
  96.3 13.5 %all-to-all-start.1 = ((f32[8,2,1,96]{3,1,2,0:T(2,128)}), f32[8,2,1,96]{3,1,2,0:T(2,128)S(1)}, u32[]{:S(2)}, u32[]{:S(2)}) async-start(f32[8,2,1,96]{3,1,2,0:T(2,128)} %constant_dynamic-update-slice_fusion.2), calls=%async_computation.1 | async-start | bytes 16384 | tf_op jit(solution)/shard_map/all_to_all | solution.py:16
  110.8 13.9 %collective-permute-start.7 = (f32[3,2,192,128]{3,2,1,0:T(8,128)S(1)}, f32[3,2,192,128]{3,2,1,0:T(8,128)S(1)}, u32[]{:S(2)}, u32[]{:S(2)}) collective-permute-start(f32[3,2,192,128]{3,2,1,0:T(8,128)S(1)} %multiply_subtract_fusion.6), channel_id=1, source_target_pairs={{8,0},{16,8},{24,16},{32,24},{40,32},{48,40},{56,48},{64,56},{72,6... | collective-permute-start | bytes 1769480 | tf_op jit(solution)/shard_map/ppermute | solution.py:30
  112.7 14.5 %collective-permute-start.6 = (f32[3,2,192,128]{3,2,1,0:T(8,128)S(1)}, f32[3,2,192,128]{3,2,1,0:T(8,128)S(1)}, u32[]{:S(2)}, u32[]{:S(2)}) collective-permute-start(f32[3,2,192,128]{3,2,1,0:T(8,128)S(1)} %multiply_subtract_fusion.6), channel_id=1, source_target_pairs={{0,8},{8,16},{16,24},{24,32},{32,40},{40,48},{48,56},{56,64},{64,7... | collective-permute-start | bytes 1769480 | tf_op jit(solution)/shard_map/ppermute | solution.py:28
  115.8 6.2 %collective-permute-start.4 = (f32[3,2,2,128]{3,2,1,0:T(2,128)S(1)}, f32[3,2,2,128]{3,2,1,0:T(2,128)S(1)}, u32[]{:S(2)}, u32[]{:S(2)}) collective-permute-start(f32[3,2,2,128]{3,2,1,0:T(2,128)S(1)} %get-tuple-element.129), channel_id=1, source_target_pairs={{1,0},{2,1},{3,2},{4,3},{5,4},{6,5},{7,6},{9,8},{10,9},{11,10},{12... | collective-permute-start | bytes 18440 | tf_op jit(solution)/shard_map/ppermute | solution.py:30
  119.2 5.5 %collective-permute-start.5 = (f32[3,2,2,128]{3,2,1,0:T(2,128)S(1)}, f32[3,2,2,128]{3,2,1,0:T(2,128)S(1)}, u32[]{:S(2)}, u32[]{:S(2)}) collective-permute-start(f32[3,2,2,128]{3,2,1,0:T(2,128)S(1)} %get-tuple-element.128), channel_id=1, source_target_pairs={{0,1},{1,2},{2,3},{3,4},{4,5},{5,6},{6,7},{8,9},{9,10},{10,11},{11... | collective-permute-start | bytes 18440 | tf_op jit(solution)/shard_map/ppermute | solution.py:28
  130.4 23.6 %all-to-all-start.2 = ((f32[2,8,96]{2,0,1:T(2,128)}), f32[2,8,96]{2,0,1:T(2,128)S(1)}, u32[]{:S(2)}, u32[]{:S(2)}) async-start(f32[2,8,96]{2,0,1:T(2,128)} %pad_maximum_fusion.12), calls=%async_computation.2 | async-start | bytes 16384 | tf_op jit(solution)/shard_map/all_to_all | solution.py:136
  139.5 36.6 %copy-start.17 = (f32[1,192]{1,0:T(1,128)S(1)}, f32[1,192]{1,0:T(1,128)}, u32[]{:S(2)}) copy-start(f32[1,192]{1,0:T(1,128)} %get-tuple-element.260) | copy-start | bytes 2308
  177.0 13.9 %collective-permute-start.11 = (f32[3,2,192,128]{3,2,1,0:T(8,128)S(1)}, f32[3,2,192,128]{3,2,1,0:T(8,128)S(1)}, u32[]{:S(2)}, u32[]{:S(2)}) collective-permute-start(f32[3,2,192,128]{3,2,1,0:T(8,128)S(1)} %multiply_subtract_fusion.5), channel_id=1, source_target_pairs={{8,0},{16,8},{24,16},{32,24},{40,32},{48,40},{56,48},{64,56},{72,6... | collective-permute-start | bytes 1769480 | tf_op jit(solution)/shard_map/ppermute | solution.py:30
  178.9 14.5 %collective-permute-start.10 = (f32[3,2,192,128]{3,2,1,0:T(8,128)S(1)}, f32[3,2,192,128]{3,2,1,0:T(8,128)S(1)}, u32[]{:S(2)}, u32[]{:S(2)}) collective-permute-start(f32[3,2,192,128]{3,2,1,0:T(8,128)S(1)} %multiply_subtract_fusion.5), channel_id=1, source_target_pairs={{0,8},{8,16},{16,24},{24,32},{32,40},{40,48},{48,56},{56,64},{64,7... | collective-permute-start | bytes 1769480 | tf_op jit(solution)/shard_map/ppermute | solution.py:28
  182.0 6.4 %collective-permute-start.8 = (f32[3,2,2,128]{3,2,1,0:T(2,128)S(1)}, f32[3,2,2,128]{3,2,1,0:T(2,128)S(1)}, u32[]{:S(2)}, u32[]{:S(2)}) collective-permute-start(f32[3,2,2,128]{3,2,1,0:T(2,128)S(1)} %get-tuple-element.113), channel_id=1, source_target_pairs={{1,0},{2,1},{3,2},{4,3},{5,4},{6,5},{7,6},{9,8},{10,9},{11,10},{12... | collective-permute-start | bytes 18440 | tf_op jit(solution)/shard_map/ppermute | solution.py:30
  185.3 5.5 %collective-permute-start.9 = (f32[3,2,2,128]{3,2,1,0:T(2,128)S(1)}, f32[3,2,2,128]{3,2,1,0:T(2,128)S(1)}, u32[]{:S(2)}, u32[]{:S(2)}) collective-permute-start(f32[3,2,2,128]{3,2,1,0:T(2,128)S(1)} %get-tuple-element.112), channel_id=1, source_target_pairs={{0,1},{1,2},{2,3},{3,4},{4,5},{5,6},{6,7},{8,9},{9,10},{10,11},{11... | collective-permute-start | bytes 18440 | tf_op jit(solution)/shard_map/ppermute | solution.py:28
  196.5 23.4 %all-to-all-start.4 = ((f32[2,8,96]{2,0,1:T(2,128)}), f32[2,8,96]{2,0,1:T(2,128)S(1)}, u32[]{:S(2)}, u32[]{:S(2)}) async-start(f32[2,8,96]{2,0,1:T(2,128)} %pad_maximum_fusion.13), calls=%async_computation.4 | async-start | bytes 16384 | tf_op jit(solution)/shard_map/all_to_all | solution.py:136
  (13 other events, 14.0 us)
